TPU v7x, 256 devices: a whole 4x4x8 slice. The times are simulated.
256 devices in a mesh: chrom: 4 (over x), snp: 64 (over z, y, core).
Axes of the slice: x: 4, y: 4, z: 8, core: 2. Of those that a mesh axis runs over, the one named last changes fastest.
Arguments:
- genotypes: bfloat16 [12288, 131072], P(None, ('chrom', 'snp')), may hold values from 0 to 2, as said below
- probes: bfloat16 [131072, 128], P(('chrom', 'snp')), may hold values from -4 to 4
Outputs:
- unit_basis: float32 [131072, 128], P(('chrom', 'snp'))
- range_log_norms: float32 [128], replicated
Inputs may be any that keep to these rules, and one draw needn't show every extreme that they name: `genotypes`: every entry is a dosage 0, 1 or 2.
All inputs are finite; a program needn't handle non-finite values.
Results may differ from a plain program's by a relative error of at most 0.0034.
The roundings to bfloat16 on the way count: a program that leaves them out, or rounds other values in their place, can miss the bound.
Values sent between devices are 32-bit elements; how exact they have to be, the bound alone decides.
No kernel may reach another device: no remote copies, remote signals or barrier semaphores. Data moves between devices by JAX's collectives and lax.ppermute only.
A program may use at most 128 MiB of HBM per device.

v0:
```python
import math
import jax
import jax.numpy as jnp
from jax import lax
from jax.sharding import PartitionSpec as P


def standardize(block):
    values = block.astype(jnp.float32)
    column_mean = jnp.mean(values, axis=0, keepdims=True)
    centered = values - column_mean
    spread = jnp.mean(centered * centered, axis=0, keepdims=True)
    return (centered * (spread + 1e-05) ** (-0.125)).astype(jnp.bfloat16)


def split_parts(sketch):
    sketch_high = lax.optimization_barrier(sketch.astype(jnp.bfloat16))
    remainder = sketch - sketch_high.astype(jnp.float32)
    sketch_mid = lax.optimization_barrier(remainder.astype(jnp.bfloat16))
    sketch_low = (remainder - sketch_mid.astype(jnp.float32)).astype(jnp.bfloat16)
    return jnp.concatenate([sketch_high, sketch_mid, sketch_low], axis=1)


def column_gram(matrix):
    return lax.dot_general(
        matrix,
        matrix,
        (((0,), (0,)), ((), ())),
        precision=lax.Precision.HIGHEST,
        preferred_element_type=jnp.float32,
    )


def unit_columns(matrix, gram_matrix):
    lower_factor = jnp.linalg.cholesky(gram_matrix)
    return lax.linalg.triangular_solve(
        lower_factor, matrix, left_side=False, lower=True, transpose_a=True
    )


def body(genotypes, probes):
    scaled = standardize(genotypes)
    width = probes.shape[1]
    partial_sketch = jnp.dot(scaled, probes, preferred_element_type=jnp.float32)
    sketch = lax.psum(partial_sketch, ("chrom", "snp"))
    sketch_parts = split_parts(sketch)
    product = lax.dot_general(
        scaled, sketch_parts, (((0,), (0,)), ((), ())), preferred_element_type=jnp.float32
    )
    range_rows = product[:, :width] + product[:, width : 2 * width] + product[:, 2 * width :]
    total_snps = range_rows.shape[0] * lax.axis_size("chrom") * lax.axis_size("snp")
    gram_first = lax.psum(column_gram(range_rows), ("chrom", "snp"))
    range_log_norms = 0.1 * jnp.log(jnp.diagonal(gram_first) / total_snps)
    first_basis = unit_columns(range_rows, gram_first)
    gram_second = lax.psum(column_gram(first_basis), ("chrom", "snp"))
    second_basis = unit_columns(first_basis, gram_second)
    return (second_basis * math.sqrt(total_snps), range_log_norms)


def solution(mesh):
    return jax.shard_map(
        body,
        mesh=mesh,
        in_specs=(P(None, ("chrom", "snp")), P(("chrom", "snp"), None)),
        out_specs=(P(("chrom", "snp"), None), P()),
        check_vma=False,
    )
```

profile of v0, /device:TPU:1, one launch (start us, length us, event | category | flops | bytes accessed | tf_op | source)
XLA Modules:
  0.0 860.5 jit_solution(15291087792489266892)
XLA Ops:
  7.2 0.0 copy-start
  7.2 0.0 all-reduce.4.cloned.1.call-start
  7.2 0.0 copy-start.2
  7.2 7.9 convert_reduce_fusion
  15.2 0.4 copy-done.2
  15.6 3.6 fusion.2
  19.2 0.0 copy-done
  19.2 5.3 fusion.6
  24.5 0.0 all-reduce.4.cloned.1.call-update
  24.5 0.0 all-reduce.6.cloned.1.call-start
  24.6 277.4 %all-reduce.4.cloned.1.call-done = f32[12288,128]{1,0:T(8,128)} async-done(((f32[12288,128]{1,0:T(8,128)}), f32[12288,128]{1,0:T(8,128)}) %all-reduce.4.cloned.1.call-update) | async-done | bytes 6291472 | tf_op jit(solution)/shard_map/psum | solution.py:45
  302.0 0.0 copy-start.1
  302.0 3.2 convert_element_type.23
  305.1 1.5 copy-done.1
  306.6 0.8 fusion.13
  307.5 1.3 subtract_convert_fusion
  308.7 11.3 %fusion.4 = f32[512,384]{1,0:T(8,128)S(1)} fusion(bf16[12288,512]{1,0:T(8,128)(2,1)} %param.5, f32[512]{0:T(512)S(1)} %add_power_fusion, f32[512]{0:T(512)S(1)} %broadcast_multiply_fusion, bf16[12288,128]{1,0:T(8,128)(2,1)S(1)} %subtract_convert_fusion, bf16[12288,128]{1,0:T(8,128)(2,1)S(1)} %fusion.13, bf16[12288,128]{1,0:T(8,128)(2,1)S(1)} %convert_element_type.23), kind=kOutput, calls=%fused_computation.7 | convolution fusion | flops 4885315584 | bytes 22810624 | tf_op jit(solution)/shard_map/dot_general | solution.py:47
  320.1 1.2 fusion.24
  321.3 0.0 all-reduce.6.cloned.1.call-update
  321.3 0.2 all-reduce.8.cloned.1.call-start
  321.6 242.2 %all-reduce.6.cloned.1.call-done = f32[128,128]{0,1:T(8,128)} async-done(((f32[128,128]{0,1:T(8,128)}), f32[128,128]{0,1:T(8,128)}) %all-reduce.6.cloned.1.call-update) | async-done | bytes 65552 | tf_op jit(solution)/shard_map/psum | solution.py:52
  563.8 0.9 copy.10
  564.8 0.9 fusion.20
  565.6 11.7 %cholesky.44 = f32[128,128]{1,0:T(8,128)S(1)} custom-call(f32[128,128]{1,0:T(8,128)S(1)} %fusion.20), custom_call_target="Cholesky" | custom-call | tf_op jit(solution)/shard_map/jit(cholesky)/cholesky | solution.py:35
  577.4 0.6 compare_reduce_fusion.1
  578.0 0.7 fusion.15
  578.7 9.8 %custom-call.8 = f32[1,128,128]{1,2,0:T(8,128)S(1)} custom-call(f32[1,128,128]{2,1,0:T(8,128)S(1)} %fusion.15), custom_call_target="InvertDiagBlocksLowerTriangular" | custom-call | tf_op jit(solution)/shard_map/triangular_solve/custom-call.0 | solution.py:36
  588.5 0.4 convolution_bitcast_fusion.1
  588.9 1.0 fusion.25
  589.9 0.0 all-reduce.8.cloned.1.call-update
  590.0 1.9 gather_fusion
  591.9 0.5 log_multiply_fusion
  592.4 235.7 %all-reduce.8.cloned.1.call-done = f32[128,128]{0,1:T(8,128)} async-done(((f32[128,128]{0,1:T(8,128)}), f32[128,128]{0,1:T(8,128)}) %all-reduce.8.cloned.1.call-update) | async-done | bytes 65552 | tf_op jit(solution)/shard_map/psum | solution.py:55
  828.1 0.9 copy.12
  829.0 0.9 fusion.18
  829.9 11.7 %cholesky.55 = f32[128,128]{1,0:T(8,128)S(1)} custom-call(f32[128,128]{1,0:T(8,128)S(1)} %fusion.18), custom_call_target="Cholesky" | custom-call | tf_op jit(solution)/shard_map/jit(cholesky)/cholesky | solution.py:35
  841.6 0.6 compare_reduce_fusion
  842.3 0.7 fusion.16
  842.9 9.8 %custom-call.9 = f32[1,128,128]{1,2,0:T(8,128)S(1)} custom-call(f32[1,128,128]{2,1,0:T(8,128)S(1)} %fusion.16), custom_call_target="InvertDiagBlocksLowerTriangular" | custom-call | tf_op jit(solution)/shard_map/triangular_solve/custom-call.0 | solution.py:36
  852.7 0.4 fusion.14
  853.2 0.8 copy.13
  (5 shorter events, 0.1 us)
Async XLA Ops:
  7.2 12.0 %copy-start = (bf16[512,128]{1,0:T(8,128)(2,1)S(1)}, bf16[512,128]{1,0:T(8,128)(2,1)}, u32[]{:S(2)}) copy-start(bf16[512,128]{1,0:T(8,128)(2,1)} %param.6) | copy-start | bytes 393220
  7.2 294.8 %all-reduce.4.cloned.1.call-start = ((), (), s32[]{:S(2)}) async-start(), calls=%async_computation | async-start | bytes 12582912 | tf_op jit(solution)/shard_map/psum | solution.py:45
  7.2 8.4 copy-start.2
  24.5 539.3 %all-reduce.6.cloned.1.call-start = ((), (), s32[]{:S(2)}) async-start(), calls=%async_computation.1 | async-start | bytes 131072 | tf_op jit(solution)/shard_map/psum | solution.py:52
  302.0 4.6 copy-start.1
  321.3 506.8 %all-reduce.8.cloned.1.call-start = ((), (), s32[]{:S(2)}) async-start(), calls=%async_computation.2 | async-start | bytes 131072 | tf_op jit(solution)/shard_map/psum | solution.py:55
Sparse Core Ops, SparseCore 0:
  24.6 277.2 all-reduce.3
  321.5 242.3 all-reduce.5
  590.1 237.9 all-reduce.7
where the time goes:
time: 861 us
  waiting for transfers between devices  755 us (88%)
  other arithmetic  64.7 us (8%)
  matrix products  19.7 us (2%)
  between operations  13.9 us (2%)
    psum x1, waiting for transfers between devices, body(): sketch = lax.psum(partial_sketch, ('chrom', 'snp'))  277 us
    psum x1, waiting for transfers between devices, body(): gram_first = lax.psum(column_gram(range_rows), ('chrom', 'snp'))  242 us
    psum x1, waiting for transfers between devices, body(): gram_second = lax.psum(column_gram(first_basis), ('chrom', 'snp'))  236 us
    another operation x6, other arithmetic, unit_columns(): lower_factor = jnp.linalg.cholesky(gram_matrix)  24.8 us
    another operation x4, other arithmetic, unit_columns(): lax.linalg.triangular_solve(lower_factor, matrix, left_side=False, lower=...  20.9 us
  transfers between devices with their start and end apart: 3, of which 3 were waited for; matrix products, arithmetic and copies ran while one was open for 0% of the time, Pallas kernels for 0%

commit v1 on v0

--- a/solution.py
+++ b/solution.py
@@ -49,7 +49,8 @@
     )
     range_rows = product[:, :width] + product[:, width : 2 * width] + product[:, 2 * width :]
     total_snps = range_rows.shape[0] * lax.axis_size("chrom") * lax.axis_size("snp")
-    gram_first = lax.psum(column_gram(range_rows), ("chrom", "snp"))
+    one_axis = lax.psum(column_gram(range_rows), "snp")
+    gram_first = lax.psum(one_axis, "chrom")
     range_log_norms = 0.1 * jnp.log(jnp.diagonal(gram_first) / total_snps)
     first_basis = unit_columns(range_rows, gram_first)
     gram_second = lax.psum(column_gram(first_basis), ("chrom", "snp"))

time: 861 us -> 840 us (0.976)
  waiting for transfers between devices: 755 us -> 734 us
    psum x1 -> x2, waiting for transfers between devices: 242 us -> 215 us  [the longest x1 172 us: body(): one_axis = lax.psum(column_gram(range_rows), 'snp')]
  transfers between devices with their start and end apart: 3 -> 4, of which waited for: 3 -> 4; matrix products, arithmetic and copies ran while one was open for 0% -> 0% of each run, Pallas kernels for 0% -> 0%
where the time goes in v1:
time: 840 us; the launch traced here: 839 us
  waiting for transfers between devices  734 us (87%)
  other arithmetic  64.7 us (8%)
  matrix products  19.7 us (2%)
  between operations  13.9 us (2%)
    psum x1, waiting for transfers between devices, body(): sketch = lax.psum(partial_sketch, ('chrom', 'snp'))  277 us
    psum x1, waiting for transfers between devices, body(): gram_second = lax.psum(column_gram(first_basis), ('chrom', 'snp'))  242 us
    psum x1, waiting for transfers between devices, body(): one_axis = lax.psum(column_gram(range_rows), 'snp')  172 us
    psum x1, waiting for transfers between devices, body(): gram_first = lax.psum(one_axis, 'chrom')  43 us
    another operation x6, other arithmetic, unit_columns(): lower_factor = jnp.linalg.cholesky(gram_matrix)  24.8 us
    another operation x4, other arithmetic, unit_columns(): lax.linalg.triangular_solve(lower_factor, matrix, left_side=False, lower=...  20.9 us
  transfers between devices with their start and end apart: 4, of which 4 were waited for; matrix products, arithmetic and copies ran while one was open for 0% of the time, Pallas kernels for 0%

profile of v1, /device:TPU:1, one launch (start us, length us, event | category | flops | bytes accessed | tf_op | source)
XLA Modules:
  0.0 839.2 jit_solution(18298855735481685165)
XLA Ops:
  7.2 0.0 copy-start
  7.2 0.0 all-reduce.5.cloned.1.call-start
  7.2 0.0 copy-start.2
  7.2 7.9 convert_reduce_fusion
  15.2 0.4 copy-done.2
  15.6 3.6 fusion.2
  19.2 0.0 copy-done
  19.2 5.3 fusion.6
  24.5 0.0 all-reduce.5.cloned.1.call-update
  24.5 0.0 all-reduce.7.cloned.1.call-start
  24.6 277.4 %all-reduce.5.cloned.1.call-done = f32[12288,128]{1,0:T(8,128)} async-done(((f32[12288,128]{1,0:T(8,128)}), f32[12288,128]{1,0:T(8,128)}) %all-reduce.5.cloned.1.call-update) | async-done | bytes 6291472 | tf_op jit(solution)/shard_map/psum | solution.py:45
  302.0 0.0 copy-start.1
  302.0 3.2 convert_element_type.23
  305.1 1.5 copy-done.1
  306.6 0.8 fusion.13
  307.5 1.3 subtract_convert_fusion
  308.7 11.3 %fusion.4 = f32[512,384]{1,0:T(8,128)S(1)} fusion(bf16[12288,512]{1,0:T(8,128)(2,1)} %param.5, f32[512]{0:T(512)S(1)} %add_power_fusion, f32[512]{0:T(512)S(1)} %broadcast_multiply_fusion, bf16[12288,128]{1,0:T(8,128)(2,1)S(1)} %subtract_convert_fusion, bf16[12288,128]{1,0:T(8,128)(2,1)S(1)} %fusion.13, bf16[12288,128]{1,0:T(8,128)(2,1)S(1)} %convert_element_type.23), kind=kOutput, calls=%fused_computation.7 | convolution fusion | flops 4885315584 | bytes 22810624 | tf_op jit(solution)/shard_map/dot_general | solution.py:47
  320.1 1.2 fusion.24
  321.3 0.0 all-reduce.7.cloned.1.call-update
  321.3 0.0 all-reduce.9.cloned.1.call-start
  321.4 171.7 %all-reduce.7.cloned.1.call-done = f32[128,128]{0,1:T(8,128)} async-done(((f32[128,128]{0,1:T(8,128)}), f32[128,128]{0,1:T(8,128)}) %all-reduce.7.cloned.1.call-update) | async-done | bytes 65552 | tf_op jit(solution)/shard_map/psum | solution.py:52
  493.1 0.0 all-reduce.9.cloned.1.call-update
  493.1 0.2 all-reduce.11.cloned.1.call-start
  493.3 43.0 %all-reduce.9.cloned.1.call-done = f32[128,128]{0,1:T(8,128)} async-done(((f32[128,128]{0,1:T(8,128)}), f32[128,128]{0,1:T(8,128)}) %all-reduce.9.cloned.1.call-update) | async-done | bytes 65552 | tf_op jit(solution)/shard_map/psum | solution.py:53
  536.3 0.9 copy.10
  537.3 0.9 fusion.20
  538.1 11.7 %cholesky.44 = f32[128,128]{1,0:T(8,128)S(1)} custom-call(f32[128,128]{1,0:T(8,128)S(1)} %fusion.20), custom_call_target="Cholesky" | custom-call | tf_op jit(solution)/shard_map/jit(cholesky)/cholesky | solution.py:35
  549.9 0.6 compare_reduce_fusion.1
  550.5 0.7 fusion.15
  551.2 9.8 %custom-call.8 = f32[1,128,128]{1,2,0:T(8,128)S(1)} custom-call(f32[1,128,128]{2,1,0:T(8,128)S(1)} %fusion.15), custom_call_target="InvertDiagBlocksLowerTriangular" | custom-call | tf_op jit(solution)/shard_map/triangular_solve/custom-call.0 | solution.py:36
  561.0 0.4 convolution_bitcast_fusion.1
  561.4 1.0 fusion.25
  562.4 0.0 all-reduce.11.cloned.1.call-update
  562.5 1.9 gather_fusion
  564.4 0.5 log_multiply_fusion
  564.9 241.8 %all-reduce.11.cloned.1.call-done = f32[128,128]{0,1:T(8,128)} async-done(((f32[128,128]{0,1:T(8,128)}), f32[128,128]{0,1:T(8,128)}) %all-reduce.11.cloned.1.call-update) | async-done | bytes 65552 | tf_op jit(solution)/shard_map/psum | solution.py:56
  806.8 0.9 copy.12
  807.7 0.9 fusion.18
  808.5 11.7 %cholesky.55 = f32[128,128]{1,0:T(8,128)S(1)} custom-call(f32[128,128]{1,0:T(8,128)S(1)} %fusion.18), custom_call_target="Cholesky" | custom-call | tf_op jit(solution)/shard_map/jit(cholesky)/cholesky | solution.py:35
  820.3 0.6 compare_reduce_fusion
  820.9 0.7 fusion.16
  821.6 9.8 %custom-call.9 = f32[1,128,128]{1,2,0:T(8,128)S(1)} custom-call(f32[1,128,128]{2,1,0:T(8,128)S(1)} %fusion.16), custom_call_target="InvertDiagBlocksLowerTriangular" | custom-call | tf_op jit(solution)/shard_map/triangular_solve/custom-call.0 | solution.py:36
  831.4 0.4 fusion.14
  831.8 0.8 copy.13
  (5 shorter events, 0.1 us)
Async XLA Ops:
  7.2 12.0 %copy-start = (bf16[512,128]{1,0:T(8,128)(2,1)S(1)}, bf16[512,128]{1,0:T(8,128)(2,1)}, u32[]{:S(2)}) copy-start(bf16[512,128]{1,0:T(8,128)(2,1)} %param.6) | copy-start | bytes 393220
  7.2 294.8 %all-reduce.5.cloned.1.call-start = ((), (), s32[]{:S(2)}) async-start(), calls=%async_computation | async-start | bytes 12582912 | tf_op jit(solution)/shard_map/psum | solution.py:45
  7.2 8.4 copy-start.2
  24.5 468.6 %all-reduce.7.cloned.1.call-start = ((), (), s32[]{:S(2)}) async-start(), calls=%async_computation.1 | async-start | bytes 131072 | tf_op jit(solution)/shard_map/psum | solution.py:52
  302.0 4.6 copy-start.1
  321.3 215.0 %all-reduce.9.cloned.1.call-start = ((), (), s32[]{:S(2)}) async-start(), calls=%async_computation.2 | async-start | bytes 131072 | tf_op jit(solution)/shard_map/psum | solution.py:53
  493.1 313.7 %all-reduce.11.cloned.1.call-start = ((), (), s32[]{:S(2)}) async-start(), calls=%async_computation.3 | async-start | bytes 131072 | tf_op jit(solution)/shard_map/psum | solution.py:56
Sparse Core Ops, SparseCore 0:
  24.6 277.2 all-reduce.4
  321.5 171.5 all-reduce.6
  495.4 40.8 all-reduce.8
  562.6 244.1 all-reduce.10
